TPU v7x, 256 devices: a whole 4x4x8 slice. The times are simulated.
256 devices in a mesh: seq: 32 (over x, z), head: 8 (over y, core).
Axes of the slice: x: 4, y: 4, z: 8, core: 2. Of those that a mesh axis runs over, the one named last changes fastest.
Arguments:
- tokens: bfloat16 [32768, 3072], P(('seq', 'head')), may hold values from -150 to 150
- norm_gain: float32 [3072], replicated, may hold values from 0.1 to 1.9
- w_query: bfloat16 [3072, 3072], P(None, 'head'), may hold values from -0.15625 to 0.15625
- w_key: bfloat16 [3072, 1024], P(None, 'head'), may hold values from -0.15625 to 0.15625
- w_value: bfloat16 [3072, 1024], P(None, 'head'), may hold values from -0.109375 to 0.109375
- w_out: bfloat16 [3072, 3072], P('head'), may hold values from -1.5 to 1.5
- long_cache: bfloat16 [2, 32768, 1024], P(None, 'seq', 'head'), may hold values from -244 to 244
- short_cache: bfloat16 [2, 8192, 1024], P(None, 'seq', 'head'), may hold values from -244 to 244
- slot_owner: int32 [8192], P('seq'), may hold values from -1 to 63, as said below
- new_len: int32 [64], replicated, may hold values from 2 to 1024, as said below
- cache_len: int32 [64], replicated, may hold values from 32 to 85, as said below
Outputs:
- layer_out: bfloat16 [32768, 3072], P(('seq', 'head'))
Inputs may be any that keep to these rules, and one draw needn't show every extreme that they name: `new_len`: lengths in order after the lead request's 64 tokens; they sum to 32704, and one request has exactly 1024 new tokens. `cache_len`: equals the number of short-cache slots that the request owns; one request has exactly 85. `slot_owner`: A request's slots are contiguous and lie in the block of 256 slots whose index equals that of the block of 1024 tokens holding the request's first new token.
All inputs are finite; a program needn't handle non-finite values.
Results may differ from a plain program's by a relative error of at most 0.02.
The roundings to bfloat16 on the way count: a program that leaves them out, or rounds other values in their place, can miss the bound.
Values may be sent and summed in bfloat16 or wider, within the bound.
A program may use at most 128 MiB of HBM per device.

v0:
```python
import math
import jax
import jax.numpy as jnp
from jax import lax
from jax.sharding import PartitionSpec as P

HD = 128
LEAD = 64
THETA_LOG = math.log(500000.0)


def from_behind(block, axis, distance):
    devices = range(lax.axis_size(axis))
    route = [(i - distance, i) for i in devices if i - distance in devices]
    return lax.ppermute(block, axis, route)


def rotate(field, position):
    half = field.shape[-1] // 2
    frequency = jnp.exp(jnp.arange(half, dtype=jnp.float32) * (-2.0 * THETA_LOG / field.shape[-1]))
    angle = position.astype(jnp.float32)[:, None] * frequency[None, :]
    cosine = jnp.cos(angle)[:, None, :]
    sine_part = jnp.sin(angle)[:, None, :]
    first_half = field[..., :half]
    second_half = field[..., half:]
    return jnp.concatenate(
        [
            first_half * cosine - second_half * sine_part,
            second_half * cosine + first_half * sine_part,
        ],
        axis=-1,
    )


def request_starts(new_len):
    return LEAD + jnp.cumsum(new_len) - new_len


def request_of(position_index, starts):
    passed = (starts[None, :] <= position_index[:, None]).astype(jnp.int32)
    request = jnp.sum(passed, axis=1) - 1
    return jnp.where(request < 0, starts.shape[0], request)


def position_of(position_index, request, starts, cache_len, long_len):
    number = starts.shape[0]
    select = jnp.arange(number, dtype=jnp.int32)[None, :] == request[:, None]
    begin = jnp.sum(jnp.where(select, starts[None, :], 0), axis=1)
    cached = jnp.sum(jnp.where(select, cache_len[None, :], 0), axis=1)
    return jnp.where(request == number, position_index + long_len, position_index - begin + cached)


def normalize(tokens, norm_gain):
    values = tokens.astype(jnp.float32)
    mean_square = jnp.mean(values * values, axis=-1, keepdims=True)
    return (values * lax.rsqrt(mean_square + 1e-05) * norm_gain).astype(jnp.bfloat16)


def raw_scores(queries, keys):
    return jnp.einsum("bgph,ngh->bgpn", queries, keys, preferred_element_type=jnp.float32) * (
        1.0 / math.sqrt(keys.shape[-1])
    )


def finish_state(scores, values):
    highest = jnp.max(scores, axis=-1)
    weights = jnp.exp(scores - highest[..., None])
    summed = jnp.sum(weights, axis=-1)
    mixture = jnp.einsum(
        "bgpn,ngh->bgph", weights.astype(jnp.bfloat16), values, preferred_element_type=jnp.float32
    )
    return (highest, summed, mixture)


def masked_state(queries, keys, values, valid):
    scores = jnp.where(valid[:, None, None, :], raw_scores(queries, keys), -jnp.inf)
    return finish_state(scores, values)


def plain_state(queries, keys, values):
    return finish_state(raw_scores(queries, keys), values)


def combine(former, latter):
    highest = jnp.maximum(former[0], latter[0])
    scale_former = jnp.exp(former[0] - highest)
    scale_latter = jnp.exp(latter[0] - highest)
    summed = former[1] * scale_former + latter[1] * scale_latter
    mixture = former[2] * scale_former[..., None] + latter[2] * scale_latter[..., None]
    return (highest, summed, mixture)


def on_device(
    tokens,
    norm_gain,
    w_query,
    w_key,
    w_value,
    w_out,
    long_cache,
    short_cache,
    slot_owner,
    new_len,
    cache_len,
):
    seq_index = lax.axis_index("seq")
    long_len = long_cache.shape[1] * lax.axis_size("seq")
    kv_heads = w_key.shape[1] // HD
    q_heads = w_query.shape[1] // HD
    per_kv = q_heads // kv_heads
    slots = short_cache.shape[1]
    q_width = w_query.shape[1]
    k_width = w_key.shape[1]
    earlier_slots, earlier_owner = from_behind((short_cache, slot_owner), "seq", 1)
    normed = normalize(tokens, norm_gain)
    piece = lax.all_gather(normed, "head", axis=0, tiled=True)
    projected = jnp.concatenate(
        [
            jnp.dot(piece, w_query, preferred_element_type=jnp.float32),
            jnp.dot(piece, w_key, preferred_element_type=jnp.float32),
            jnp.dot(piece, w_value, preferred_element_type=jnp.float32),
        ],
        axis=1,
    )
    local_rows = projected.shape[0]
    starts = request_starts(new_len)
    token_index = seq_index * local_rows + jnp.arange(local_rows, dtype=jnp.int32)
    request = request_of(token_index, starts)
    position = position_of(token_index, request, starts, cache_len, long_len)
    before_index = token_index - local_rows
    before_request = request_of(before_index, starts)
    queries = rotate(projected[:, :q_width].reshape(local_rows, q_heads, HD), position).astype(
        jnp.bfloat16
    )
    queries = queries.reshape(local_rows, kv_heads, per_kv, HD)
    keys = rotate(
        projected[:, q_width : q_width + k_width].reshape(local_rows, kv_heads, HD), position
    ).astype(jnp.bfloat16)
    values = projected[:, q_width + k_width :].astype(jnp.bfloat16)
    fresh = jnp.stack([keys.reshape(local_rows, k_width), values])
    earlier_fresh = from_behind(fresh, "seq", 1)
    has_before = seq_index > 0
    new_rows = jnp.concatenate([earlier_fresh, fresh], axis=1)
    new_keys = new_rows[0].reshape(-1, kv_heads, HD)
    new_values = new_rows[1].reshape(-1, kv_heads, HD)
    slot_rows = jnp.concatenate([earlier_slots, short_cache], axis=1)
    slot_keys = slot_rows[0].reshape(-1, kv_heads, HD)
    slot_values = slot_rows[1].reshape(-1, kv_heads, HD)
    new_request = jnp.concatenate([jnp.where(has_before, before_request, -1), request])
    new_index = jnp.concatenate([before_index, token_index])
    slot_request = jnp.concatenate([jnp.where(has_before, earlier_owner, -1), slot_owner]).astype(
        jnp.int32
    )
    slot_index = jnp.full((2 * slots,), -1, jnp.int32)
    block_rows = min(local_rows, 512)
    block_count = local_rows // block_rows
    window = local_rows + block_rows

    def local_block(item):
        block_queries, block_request, block_index, block_number = item
        begin = block_number * block_rows
        window_keys = jnp.concatenate(
            [lax.dynamic_slice_in_dim(new_keys, begin, window, 0), slot_keys], axis=0
        )
        window_values = jnp.concatenate(
            [lax.dynamic_slice_in_dim(new_values, begin, window, 0), slot_values], axis=0
        )
        window_request = jnp.concatenate(
            [lax.dynamic_slice_in_dim(new_request, begin, window, 0), slot_request]
        )
        window_index = jnp.concatenate(
            [lax.dynamic_slice_in_dim(new_index, begin, window, 0), slot_index]
        )
        valid = (window_request[None, :] == block_request[:, None]) & (
            window_index[None, :] <= block_index[:, None]
        )
        return masked_state(block_queries, window_keys, window_values, valid)

    highest, summed, mixture = lax.map(
        local_block,
        (
            queries.reshape(block_count, block_rows, kv_heads, per_kv, HD),
            request.reshape(block_count, block_rows),
            token_index.reshape(block_count, block_rows),
            jnp.arange(block_count, dtype=jnp.int32),
        ),
    )
    highest = highest.reshape(local_rows, kv_heads, per_kv)
    summed = summed.reshape(local_rows, kv_heads, per_kv)
    mixture = mixture.reshape(local_rows, kv_heads, per_kv, HD)
    lead_queries = queries[:LEAD]
    start_state = (
        jnp.full((LEAD, kv_heads, per_kv), -1e30, jnp.float32),
        jnp.zeros((LEAD, kv_heads, per_kv), jnp.float32),
        jnp.zeros((LEAD, kv_heads, per_kv, HD), jnp.float32),
    )
    piece = lax.all_gather(long_cache, "seq", axis=1, tiled=True)
    long_state = combine(
        start_state,
        plain_state(
            lead_queries, piece[0].reshape(-1, kv_heads, HD), piece[1].reshape(-1, kv_heads, HD)
        ),
    )
    long_highest = jnp.where(seq_index == 0, long_state[0], -1e30)
    joined = combine(
        (highest[:LEAD], summed[:LEAD], mixture[:LEAD]),
        (long_highest, long_state[1], long_state[2]),
    )
    summed = jnp.concatenate([joined[1], summed[LEAD:]], axis=0)
    mixture = jnp.concatenate([joined[2], mixture[LEAD:]], axis=0)
    attended = (mixture / summed[..., None]).astype(jnp.bfloat16).reshape(local_rows, q_width)
    gathered_sum = lax.psum_scatter(
        jnp.dot(attended, w_out, preferred_element_type=jnp.float32).astype(jnp.bfloat16),
        "head",
        scatter_dimension=0,
        tiled=True,
    )
    return gathered_sum


def solution(mesh):
    placed = (
        P(("seq", "head"), None),
        P(),
        P(None, "head"),
        P(None, "head"),
        P(None, "head"),
        P("head", None),
        P(None, "seq", "head"),
        P(None, "seq", "head"),
        P("seq"),
        P(),
        P(),
    )
    return jax.shard_map(
        on_device, mesh=mesh, in_specs=placed, out_specs=P(("seq", "head"), None), check_vma=False
    )
```

profile of v0, /device:TPU:1, one launch (start us, length us, event | category | flops | bytes accessed | tf_op | source)
XLA Modules:
  0.0 298.3 jit_solution(11702035966844528671)
XLA Ops:
  6.5 1.5 fusion.29
  8.1 2.3 fusion.31
  11.2 4.4 %collective-permute-start = (s32[256]{0:T(256)}, s32[256]{0:T(256)S(1)}, u32[]{:S(2)}, u32[]{:S(2)}) collective-permute-start(s32[256]{0:T(256)} %param.21), channel_id=1, source_target_pairs={{0,8},{8,16},{16,24},{24,32},{32,40},{40,48},{48,56},{56,64},{64,7... | collective-permute-start | bytes 3080 | tf_op jit(solution)/shard_map/ppermute | solution.py:15
  15.6 3.6 %collective-permute-start.2 = (bf16[2,256,128]{2,1,0:T(8,128)(2,1)}, bf16[2,256,128]{2,1,0:T(8,128)(2,1)S(1)}, u32[]{:S(2)}, u32[]{:S(2)}) collective-permute-start(bf16[2,256,128]{2,1,0:T(8,128)(2,1)} %param.20), channel_id=1, source_target_pairs={{0,8},{8,16},{16,24},{24,32},{32,40},{40,48},{48,56},{56,64},{64,7... | collective-permute-start | bytes 393224 | tf_op jit(solution)/shard_map/ppermute | solution.py:15
  20.9 0.8 select_reduce_fusion.1
  22.4 3.1 %multiply_cosine_fusion = (f32[1024,64]{1,0:T(8,128)}, f32[1024,64]{1,0:T(8,128)}) fusion(f32[64]{0:T(128)S(1)} %multiply_exponential_fusion, f32[1024]{0:T(1024)S(1)} %get-tuple-element.196), kind=kLoop, calls=%fused_computation.63 | loop fusion | flops 65536 | bytes 528640 | tf_op jit(solution)/shard_map/cos | solution.py:22
  28.1 30.1 %all-gather.3.cloned.1.call-done = bf16[1024,3072]{1,0:T(8,128)(2,1)} async-done(((bf16[128,3072]{1,0:T(8,128)(2,1)}), bf16[1024,3072]{1,0:T(8,128)(2,1)}) %all-gather.3.cloned.1.call-update) | async-done | bytes 6291472 | tf_op jit(solution)/shard_map/all_gather | solution.py:116
  58.3 5.3 %convolution_bitcast_fusion = f32[1024,1,128]{0,2,1:T(8,128)S(1)} fusion(bf16[1024,3072]{1,0:T(8,128)(2,1)} %all-gather.3.cloned.1.call-done, bf16[3072,128]{1,0:T(8,128)(2,1)} %param.16), kind=kOutput, calls=%fused_computation.51 | convolution fusion | flops 805306368 | bytes 7602176 | tf_op jit(solution)/shard_map/dot_general | solution.py:120
  63.6 1.2 fusion.61
  64.8 2.2 fusion.33
  67.0 0.8 pad_maximum_fusion.1
  67.9 4.0 %collective-permute-start.1 = (bf16[2,1024,128]{1,2,0:T(8,128)(2,1)}, bf16[2,1024,128]{1,2,0:T(8,128)(2,1)}, u32[]{:S(2)}, u32[]{:S(2)}) collective-permute-start(bf16[2,1024,128]{1,2,0:T(8,128)(2,1)} %pad_maximum_fusion.1), channel_id=1, source_target_pairs={{0,8},{8,16},{16,24},{24,32},{32,40},{40,48},{48,56},{56,64},{64,7... | collective-permute-start | bytes 1572872 | tf_op jit(solution)/shard_map/ppermute | solution.py:15
  71.9 2.7 fusion.76
  74.6 1.0 fusion.74
  75.6 2.8 copy.74
  78.4 1.6 copy.73
  80.0 2.6 subtract_convert_fusion
  82.6 0.9 copy-done.2
  83.6 1.3 pad_maximum_fusion
  84.9 4.6 %collective-permute-done.1 = bf16[2,1024,128]{1,2,0:T(8,128)(2,1)} collective-permute-done((bf16[2,1024,128]{1,2,0:T(8,128)(2,1)}, bf16[2,1024,128]{1,2,0:T(8,128)(2,1)}, u32[]{:S(2)}, u32[]{:S(2)}) %collective-permute-start.1) | collective-permute-done | bytes 524320 | tf_op jit(solution)/shard_map/ppermute | solution.py:15
  89.5 1.1 maximum_maximum_fusion
  90.6 1.1 slice_bitcast_fusion.16
  91.7 73.2 %while.14 = (s32[]{:T(128)}, f32[2,512,1,3]{1,0,3,2:T(2,128)}, f32[2,512,1,3]{1,0,2,3:T(2,128)}, f32[2,512,1,3,128]{4,1,0,3,2:T(8,128)}, s32[2]{0:T(128)S(1)}, /...) while((s32[]{:T(128)}, f32[2,512,1,3]{1,0,3,2:T(2,128)}, ...), condition=%wide.region_9.10_spmd, body=%wide.region_6.9_spmd.sunk | while | flops 1650459648 | bytes 50030996 | solution.py:179
  94.6 1.5 compare_and_fusion.2
  96.2 2.1 constant_dynamic-slice_fusion.7
  98.2 1.9 copy.86
  100.2 8.1 %fusion.90 = (f32[512,3]{0,1:T(4,128)S(1)}, f32[2048,512,3]{1,0,2:T(8,128)}) fusion(pred[512,2048]{0,1:T(8,128)(4,1)S(1)} %compare_and_fusion.2, bf16[2,512,1,3,128]{4,1,0,3,2:T(8,128)(2,1)} %get-tuple-element.368, s32[]{:T(128)S(6)} %copy.97, bf16[512,1,128]{2,0,1:T(8,128)(2,1)} %get-tuple-element.367, bf16[1536,1,128]{2,0,1:T(8,128)(2,1)} %copy.86), kind=kOutput, calls=%fused_computation.4.clone.1 | convolution fusion | flops 815790592 | bytes 14555140 | tf_op jit(solution)/shard_map/while/body/eval_jaxpr/bgph,ngh->bgpn/dot_general | solution.py:60
  108.4 7.3 %fusion.91 = f32[512,3]{0,1:T(4,128)S(1)} fusion(f32[2048,512,3]{1,0,2:T(8,128)} %get-tuple-element.311, f32[512,3]{0,1:T(4,128)S(1)} %get-tuple-element.310, pred[512,2048]{0,1:T(8,128)(4,1)S(1)} %compare_and_fusion.2), kind=kLoop, calls=%fused_computation.3.clone.1 | loop fusion | flops 12581376 | bytes 13643776 | tf_op jit(solution)/shard_map/while/body/eval_jaxpr/reduce_sum | solution.py:68
  115.8 10.4 %fusion.92 = f32[1,512,1,3,128]{1,4,3,2,0:T(8,128)} fusion(f32[2048,512,3]{1,0,2:T(8,128)} %get-tuple-element.311, f32[512,3]{0,1:T(4,128)S(1)} %get-tuple-element.310, pred[512,2048]{0,1:T(8,128)(4,1)S(1)} %compare_and_fusion.2, bf16[512,1,128]{0,2,1:T(8,128)(2,1)} %get-tuple-element.370, bf16[1536,1,128]{0,2,1:T(8,128)(2,1)} %get-tuple-element.312), kind=kOutput, calls=%fused_computation.9.clone.1 | convolution fusion | flops 818937856 | bytes 14948352 | tf_op jit(solution)/shard_map/while/body/eval_jaxpr/bgpn,ngh->bgph/dot_general | solution.py:69
  126.2 1.4 copy.88
  127.6 0.9 constant_dynamic-update-slice_fusion.4
  131.4 1.5 compare_and_fusion.2
  133.0 2.1 constant_dynamic-slice_fusion.7
  135.1 1.9 copy.86
  137.0 8.1 %fusion.90 = (f32[512,3]{0,1:T(4,128)S(1)}, f32[2048,512,3]{1,0,2:T(8,128)}) fusion(pred[512,2048]{0,1:T(8,128)(4,1)S(1)} %compare_and_fusion.2, bf16[2,512,1,3,128]{4,1,0,3,2:T(8,128)(2,1)} %get-tuple-element.368, s32[]{:T(128)S(6)} %copy.97, bf16[512,1,128]{2,0,1:T(8,128)(2,1)} %get-tuple-element.367, bf16[1536,1,128]{2,0,1:T(8,128)(2,1)} %copy.86), kind=kOutput, calls=%fused_computation.4.clone.1 | convolution fusion | flops 815790592 | bytes 14555140 | tf_op jit(solution)/shard_map/while/body/eval_jaxpr/bgph,ngh->bgpn/dot_general | solution.py:60
  145.2 7.6 %fusion.91 = f32[512,3]{0,1:T(4,128)S(1)} fusion(f32[2048,512,3]{1,0,2:T(8,128)} %get-tuple-element.311, f32[512,3]{0,1:T(4,128)S(1)} %get-tuple-element.310, pred[512,2048]{0,1:T(8,128)(4,1)S(1)} %compare_and_fusion.2), kind=kLoop, calls=%fused_computation.3.clone.1 | loop fusion | flops 12581376 | bytes 13643776 | tf_op jit(solution)/shard_map/while/body/eval_jaxpr/reduce_sum | solution.py:68
  152.9 9.6 %fusion.92 = f32[1,512,1,3,128]{1,4,3,2,0:T(8,128)} fusion(f32[2048,512,3]{1,0,2:T(8,128)} %get-tuple-element.311, f32[512,3]{0,1:T(4,128)S(1)} %get-tuple-element.310, pred[512,2048]{0,1:T(8,128)(4,1)S(1)} %compare_and_fusion.2, bf16[512,1,128]{0,2,1:T(8,128)(2,1)} %get-tuple-element.370, bf16[1536,1,128]{0,2,1:T(8,128)(2,1)} %get-tuple-element.312), kind=kOutput, calls=%fused_computation.9.clone.1 | convolution fusion | flops 818937856 | bytes 14948352 | tf_op jit(solution)/shard_map/while/body/eval_jaxpr/bgpn,ngh->bgph/dot_general | solution.py:69
  162.5 1.4 copy.88
  163.9 1.0 constant_dynamic-update-slice_fusion.4
  164.9 2.7 slice.77
  167.6 3.1 %copy.54 = f32[960,1,3,128]{0,3,2,1:T(8,128)} copy(f32[960,1,3,128]{3,0,2,1:T(8,128)} %slice.77) | data formatting | bytes 2949120 | tf_op jit(solution)/shard_map/slice | solution.py:210
  170.8 33.9 %all-gather.5.cloned.1.call-done = bf16[2,32768,128]{2,1,0:T(8,128)(2,1)} async-done(((bf16[2,1024,128]{2,1,0:T(8,128)(2,1)}), bf16[2,32768,128]{2,1,0:T(8,128)(2,1)}) %all-gather.5.cloned.1.call-update) | async-done | bytes 16777232 | tf_op jit(solution)/shard_map/all_gather | solution.py:197
  204.8 12.3 %fusion.75 = (f32[64,3]{0,1:T(4,128)S(1)}, f32[64,1,3,32768]{3,0,2,1:T(8,128)}) fusion(bf16[2,32768,128]{2,1,0:T(8,128)(2,1)} %all-gather.5.cloned.1.call-done, bf16[1024,3,64]{2,0,1:T(8,128)(2,1)} %copy-done.4, bf16[1024,3,64]{2,0,1:T(8,128)(2,1)S(1)} %copy-done.3), kind=kOutput, calls=%fused_computation.124 | convolution fusion | flops 1623293696 | bytes 34734848 | tf_op jit(solution)/shard_map/bgph,ngh->bgpn/dot_general | solution.py:60
  217.0 10.6 %fusion.23 = f32[64,3]{0,1:T(4,128)S(1)} fusion(f32[64,1,3,32768]{3,0,2,1:T(8,128)} %get-tuple-element.201, f32[64,3]{0,1:T(4,128)S(1)} %get-tuple-element.200), kind=kLoop, calls=%fused_computation.34 | loop fusion | flops 12582720 | bytes 25167360 | tf_op jit(solution)/shard_map/reduce_sum | solution.py:68
  227.7 14.4 %fusion.49 = f32[64,1,3,128]{3,0,2,1:T(8,128)S(1)} fusion(bf16[2,32768,128]{2,1,0:T(8,128)(2,1)} %all-gather.5.cloned.1.call-done, f32[64,1,3,32768]{3,0,2,1:T(8,128)} %get-tuple-element.201, f32[64,3]{0,1:T(4,128)S(1)} %get-tuple-element.200, f32[1024,1,3,128]{3,0,2,1:T(8,128)} %bitcast.189, f32[64,3]{0,1:T(4,128)S(1)} %bitcast.196, ...), kind=kOutput, calls=%fused_computation.59 | convolution fusion | flops 1623318528 | bytes 33754880 | tf_op jit(solution)/shard_map/bgpn,ngh->bgph/dot_general | solution.py:69
  242.4 1.9 fusion.32
  244.3 5.4 %convolution_convert_fusion = bf16[1024,3072]{1,0:T(8,128)(2,1)} fusion(bf16[1024,384]{0,1:T(8,128)(2,1)S(1)} %fusion.32, bf16[384,3072]{1,0:T(8,128)(2,1)S(1)} %copy-done), kind=kOutput, calls=%fused_computation.41 | convolution fusion | flops 2419064832 | bytes 9437184 | tf_op jit(solution)/shard_map/dot_general | solution.py:213
  249.7 42.1 %reduce-scatter.2.cloned.1.call-done = bf16[128,3072]{1,0:T(8,128)(2,1)} async-done(((bf16[1024,3072]{1,0:T(8,128)(2,1)}), bf16[128,3072]{1,0:T(8,128)(2,1)}) %reduce-scatter.2.cloned.1.call-update) | async-done | bytes 786448 | tf_op jit(solution)/shard_map/reduce_scatter | solution.py:212
  (102 shorter events, 11.0 us)
Async XLA Ops:
  6.5 237.7 %copy-start = (bf16[384,3072]{1,0:T(8,128)(2,1)S(1)}, bf16[384,3072]{1,0:T(8,128)(2,1)}, u32[]{:S(2)}) copy-start(bf16[384,3072]{1,0:T(8,128)(2,1)} %param.18) | copy-start | bytes 7077892
  6.5 20.1 %copy-start.8 = (bf16[2,256,128]{2,1,0:T(8,128)(2,1)S(1)}, bf16[2,256,128]{2,1,0:T(8,128)(2,1)}, u32[]{:S(2)}) copy-start(bf16[2,256,128]{2,1,0:T(8,128)(2,1)} %param.20) | copy-start | bytes 393220
  6.5 51.7 %all-gather.3.cloned.1.call-start = ((), (), s32[]{:S(2)}) async-start(), calls=%async_computation.1 | async-start | bytes 7077888 | tf_op jit(solution)/shard_map/all_gather | solution.py:116
  10.4 194.4 %all-gather.5.cloned.1.call-start = ((), (), s32[]{:S(2)}) async-start(), calls=%async_computation.2 | async-start | bytes 17301504 | tf_op jit(solution)/shard_map/all_gather | solution.py:197
  11.1 280.7 %reduce-scatter.2.cloned.1.call-start = ((), (), s32[]{:S(2)}) async-start(), calls=%async_computation.3 | async-start | bytes 7077888 | tf_op jit(solution)/shard_map/reduce_scatter | solution.py:212
  11.2 14.8 %collective-permute-start = (s32[256]{0:T(256)}, s32[256]{0:T(256)S(1)}, u32[]{:S(2)}, u32[]{:S(2)}) collective-permute-start(s32[256]{0:T(256)} %param.21), channel_id=1, source_target_pairs={{0,8},{8,16},{16,24},{24,32},{32,40},{40,48},{48,56},{56,64},{64,7... | collective-permute-start | bytes 3080 | tf_op jit(solution)/shard_map/ppermute | solution.py:15
  15.6 11.1 %collective-permute-start.2 = (bf16[2,256,128]{2,1,0:T(8,128)(2,1)}, bf16[2,256,128]{2,1,0:T(8,128)(2,1)S(1)}, u32[]{:S(2)}, u32[]{:S(2)}) collective-permute-start(bf16[2,256,128]{2,1,0:T(8,128)(2,1)} %param.20), channel_id=1, source_target_pairs={{0,8},{8,16},{16,24},{24,32},{32,40},{40,48},{48,56},{56,64},{64,7... | collective-permute-start | bytes 393224 | tf_op jit(solution)/shard_map/ppermute | solution.py:15
  28.1 36.6 %copy-start.7 = (bf16[3072,128]{1,0:T(8,128)(2,1)S(1)}, bf16[3072,128]{1,0:T(8,128)(2,1)}, u32[]{:S(2)}) copy-start(bf16[3072,128]{1,0:T(8,128)(2,1)} %param.17) | copy-start | bytes 2359300
  58.3 6.5 %copy-start.1 = (bf16[1024,3072]{1,0:T(8,128)(2,1)S(1)}, bf16[1024,3072]{1,0:T(8,128)(2,1)}, u32[]{:S(2)}) copy-start(bf16[1024,3072]{1,0:T(8,128)(2,1)} %all-gather.3.cloned.1.call-done) | copy-start | bytes 18874372
  64.8 2.2 copy-start.5
  64.8 7.1 %copy-start.15 = (bf16[3072,384]{1,0:T(8,128)(2,1)S(1)}, bf16[3072,384]{1,0:T(8,128)(2,1)}, u32[]{:S(2)}) copy-start(bf16[3072,384]{1,0:T(8,128)(2,1)} %param.15) | copy-start | bytes 7077892
  67.9 21.6 %collective-permute-start.1 = (bf16[2,1024,128]{1,2,0:T(8,128)(2,1)}, bf16[2,1024,128]{1,2,0:T(8,128)(2,1)}, u32[]{:S(2)}, u32[]{:S(2)}) collective-permute-start(bf16[2,1024,128]{1,2,0:T(8,128)(2,1)} %pad_maximum_fusion.1), channel_id=1, source_target_pairs={{0,8},{8,16},{16,24},{24,32},{32,40},{40,48},{48,56},{56,64},{64,7... | collective-permute-start | bytes 1572872 | tf_op jit(solution)/shard_map/ppermute | solution.py:15
  80.0 9.5 %copy-start.6 = (bf16[1,1024,64]{1,2,0:T(8,128)(2,1)S(1)}, bf16[1,1024,64]{1,2,0:T(8,128)(2,1)}, u32[]{:S(2)}) copy-start(bf16[1,1024,64]{1,2,0:T(8,128)(2,1)} %copy-done.5) | copy-start | bytes 393220
  82.6 0.9 copy-start.2
  82.6 2.2 copy-start.4
  100.2 8.1 %copy-start.9 = (f32[2,512,1,3]{1,0,3,2:T(2,128)S(1)}, f32[2,512,1,3]{1,0,3,2:T(2,128)}, u32[]{:S(2)}) copy-start(f32[2,512,1,3]{1,0,3,2:T(2,128)} %get-tuple-element.335) | copy-start | bytes 36868 | tf_op jit(solution)/shard_map/while
  108.4 7.3 %copy-start.10 = (f32[2,512,1,3]{1,0,3,2:T(2,128)}, f32[2,512,1,3]{1,0,3,2:T(2,128)S(1)}, u32[]{:S(2)}) copy-start(f32[2,512,1,3]{1,0,3,2:T(2,128)S(1)} %dynamic_update_slice.16) | copy-start | bytes 36868 | tf_op jit(solution)/shard_map/while
  108.4 7.3 %copy-start.12 = (f32[2,512,1,3]{1,0,2,3:T(2,128)S(1)}, f32[2,512,1,3]{1,0,2,3:T(2,128)}, u32[]{:S(2)}) copy-start(f32[2,512,1,3]{1,0,2,3:T(2,128)} %get-tuple-element.336) | copy-start | bytes 36868 | tf_op jit(solution)/shard_map/while
  115.8 10.4 %copy-start.13 = (f32[2,512,1,3]{1,0,2,3:T(2,128)}, f32[2,512,1,3]{1,0,2,3:T(2,128)S(1)}, u32[]{:S(2)}) copy-start(f32[2,512,1,3]{1,0,2,3:T(2,128)S(1)} %dynamic_update_slice.17) | copy-start | bytes 36868 | tf_op jit(solution)/shard_map/while
  137.0 8.1 %copy-start.9 = (f32[2,512,1,3]{1,0,3,2:T(2,128)S(1)}, f32[2,512,1,3]{1,0,3,2:T(2,128)}, u32[]{:S(2)}) copy-start(f32[2,512,1,3]{1,0,3,2:T(2,128)} %get-tuple-element.335) | copy-start | bytes 36868 | tf_op jit(solution)/shard_map/while
  145.2 7.6 %copy-start.10 = (f32[2,512,1,3]{1,0,3,2:T(2,128)}, f32[2,512,1,3]{1,0,3,2:T(2,128)S(1)}, u32[]{:S(2)}) copy-start(f32[2,512,1,3]{1,0,3,2:T(2,128)S(1)} %dynamic_update_slice.16) | copy-start | bytes 36868 | tf_op jit(solution)/shard_map/while
  145.2 7.6 %copy-start.12 = (f32[2,512,1,3]{1,0,2,3:T(2,128)S(1)}, f32[2,512,1,3]{1,0,2,3:T(2,128)}, u32[]{:S(2)}) copy-start(f32[2,512,1,3]{1,0,2,3:T(2,128)} %get-tuple-element.336) | copy-start | bytes 36868 | tf_op jit(solution)/shard_map/while
  152.9 9.6 %copy-start.13 = (f32[2,512,1,3]{1,0,2,3:T(2,128)}, f32[2,512,1,3]{1,0,2,3:T(2,128)S(1)}, u32[]{:S(2)}) copy-start(f32[2,512,1,3]{1,0,2,3:T(2,128)S(1)} %dynamic_update_slice.17) | copy-start | bytes 36868 | tf_op jit(solution)/shard_map/while
  164.9 5.8 %copy-start.14 = (f32[2,512,1,3]{1,0,2,3:T(2,128)S(1)}, f32[2,512,1,3]{1,0,2,3:T(2,128)}, u32[]{:S(2)}) copy-start(f32[2,512,1,3]{1,0,2,3:T(2,128)} %get-tuple-element.91) | copy-start | bytes 36868
  164.9 5.8 %copy-start.11 = (f32[2,512,1,3]{1,0,3,2:T(2,128)S(1)}, f32[2,512,1,3]{1,0,3,2:T(2,128)}, u32[]{:S(2)}) copy-start(f32[2,512,1,3]{1,0,3,2:T(2,128)} %get-tuple-element.90) | copy-start | bytes 36868
  164.9 39.9 %copy-start.3 = (bf16[1024,3,64]{2,0,1:T(8,128)(2,1)S(1)}, bf16[1024,3,64]{2,0,1:T(8,128)(2,1)}, u32[]{:S(2)}) copy-start(bf16[1024,3,64]{2,0,1:T(8,128)(2,1)} %copy-done.2) | copy-start | bytes 1179652
Sparse Core Ops, SparseCore 0:
  10.5 47.6 all-gather.2
  60.8 143.8 all-gather.4
  249.8 41.9 reduce-scatter.1
where the time goes:
time: 299 us; the launch traced here: 298 us
  waiting for transfers between devices  111 us (37%)
  matrix products  78.4 us (26%)
  other arithmetic  49.5 us (17%)
  local copies, waits for them, and re-layouts  31.9 us (11%)
  between operations  13.4 us (4%)
  starting transfers between devices  12 us (4%)
    reduce_scatter x1, waiting for transfers between devices, on_device(): lax.psum_scatter(jnp.dot(attended, w_out, preferred_element_type=jnp.floa...  42.1 us
    dot_general x3, matrix products, finish_state(): jnp.einsum('bgpn,ngh->bgph', weights.astype(jnp.bfloat16), values, prefer...  34.4 us
    all_gather x1, waiting for transfers between devices, on_device(): piece = lax.all_gather(long_cache, 'seq', axis=1, tiled=True)  33.9 us
    all_gather x1, waiting for transfers between devices, on_device(): piece = lax.all_gather(normed, 'head', axis=0, tiled=True)  30.1 us
    dot_general x3, matrix products, raw_scores(): jnp.einsum('bgph,ngh->bgpn', queries, keys, preferred_element_type=jnp.fl...  28.4 us
    reduce_sum x3, other arithmetic, finish_state(): summed = jnp.sum(weights, axis=-1)  25.5 us
    ppermute x3, starting transfers between devices, from_behind(): return lax.ppermute(block, axis, route)  11.9 us
  transfers between devices with their start and end apart: 6, of which 4 were waited for; matrix products, arithmetic and copies ran while one was open for 37% of the time, Pallas kernels for 0%

commit v1 on v0

--- a/solution.py
+++ b/solution.py
@@ -113,7 +113,12 @@
     k_width = w_key.shape[1]
     earlier_slots, earlier_owner = from_behind((short_cache, slot_owner), "seq", 1)
     normed = normalize(tokens, norm_gain)
-    piece = lax.all_gather(normed, "head", axis=0, tiled=True)
+    ring = [normed]
+    for hop in range(7):
+        ring.append(lax.ppermute(ring[-1], "head", [(dev, (dev + 1) % 8) for dev in range(8)]))
+    piece = jnp.roll(
+        jnp.concatenate(ring[::-1], axis=0), (lax.axis_index("head") + 1) * ring[0].shape[0], axis=0
+    )
     projected = jnp.concatenate(
         [
             jnp.dot(piece, w_query, preferred_element_type=jnp.float32),

time: 299 us -> 325 us (1.087)
  starting transfers between devices: 12 us -> 28.5 us
  local copies, waits for them, and re-layouts: 31.9 us -> 47.5 us
  matrix products: 78.4 us -> 74.3 us
  other arithmetic: 49.5 us -> 45.7 us
    ppermute x0 -> x7, waiting for transfers between devices: none -> 49.2 us  [on_device(): lax.ppermute(ring[-1], 'head', [(dev, (dev + 1) % 8) for dev in range(8)])]
    all_gather x1, waiting for transfers between devices: 33.9 us -> 0.02 us  [on_device(): piece = lax.all_gather(long_cache, 'seq', axis=1, tiled=True)]
    all_gather x1 -> x0, waiting for transfers between devices: 30.1 us -> none  [on_device(): piece = lax.all_gather(normed, 'head', axis=0, tiled=True)]
    ppermute x0 -> x7, starting transfers between devices: none -> 17.7 us  [on_device(): lax.ppermute(ring[-1], 'head', [(dev, (dev + 1) % 8) for dev in range(8)])]
    unnamed x30 -> x48, local copies, waits for them, and re-layouts: 5.37 us -> 21.8 us
    reduce_scatter x1, waiting for transfers between devices: 42.1 us -> 56.6 us  [on_device(): lax.psum_scatter(jnp.dot(attended, w_out, preferred_element_type=jnp.floa...]
  transfers between devices with their start and end apart: 6 -> 12, of which waited for: 4 -> 9; matrix products, arithmetic and copies ran while one was open for 37% -> 37% of each run, Pallas kernels for 0% -> 0%
where the time goes in v1:
time: 325 us; the launch traced here: 324 us
  waiting for transfers between devices  113 us (35%)
  matrix products  74.3 us (23%)
  local copies, waits for them, and re-layouts  47.5 us (15%)
  other arithmetic  45.7 us (14%)
  starting transfers between devices  28.5 us (9%)
  between operations  13.8 us (4%)
    reduce_scatter x1, waiting for transfers between devices, on_device(): lax.psum_scatter(jnp.dot(attended, w_out, preferred_element_type=jnp.floa...  56.6 us
    ppermute x7, waiting for transfers between devices, on_device(): lax.ppermute(ring[-1], 'head', [(dev, (dev + 1) % 8) for dev in range(8)])  49.2 us
    dot_general x3, matrix products, finish_state(): jnp.einsum('bgpn,ngh->bgph', weights.astype(jnp.bfloat16), values, prefer...  33 us
    dot_general x3, matrix products, raw_scores(): jnp.einsum('bgph,ngh->bgpn', queries, keys, preferred_element_type=jnp.fl...  28.6 us
    reduce_sum x3, other arithmetic, finish_state(): summed = jnp.sum(weights, axis=-1)  25.2 us
    unnamed x48, local copies, waits for them, and re-layouts  21.8 us
    ppermute x7, starting transfers between devices, on_device(): lax.ppermute(ring[-1], 'head', [(dev, (dev + 1) % 8) for dev in range(8)])  17.7 us
    ppermute x3, starting transfers between devices, from_behind(): return lax.ppermute(block, axis, route)  10.7 us
  transfers between devices with their start and end apart: 12, of which 9 were waited for; matrix products, arithmetic and copies ran while one was open for 37% of the time, Pallas kernels for 0%

profile of v1, /device:TPU:1, one launch (start us, length us, event | category | flops | bytes accessed | tf_op | source)
XLA Modules:
  0.0 323.8 jit_solution(10707929959841465008)
XLA Ops:
  7.3 1.4 fusion.35
  8.7 1.4 fusion.37
  10.1 2.7 collective-permute-start.1
  12.8 8.9 %collective-permute-done.1 = bf16[128,3072]{1,0:T(8,128)(2,1)S(1)} collective-permute-done((bf16[128,3072]{1,0:T(8,128)(2,1)S(1)}, bf16[128,3072]{1,0:T(8,128)(2,1)S(1)}, u32[]{:S(2)}, u32[]{:S(2)}) %collective-permute-start.1) | collective-permute-done | bytes 786464 | tf_op jit(solution)/shard_map/ppermute | solution.py:118
  22.6 2.5 collective-permute-start.2
  25.1 8.9 %collective-permute-done.2 = bf16[128,3072]{1,0:T(8,128)(2,1)S(1)} collective-permute-done((bf16[128,3072]{1,0:T(8,128)(2,1)S(1)}, bf16[128,3072]{1,0:T(8,128)(2,1)S(1)}, u32[]{:S(2)}, u32[]{:S(2)}) %collective-permute-start.2) | collective-permute-done | bytes 786464 | tf_op jit(solution)/shard_map/ppermute | solution.py:118
  34.9 2.5 collective-permute-start.3
  37.4 8.9 %collective-permute-done.3 = bf16[128,3072]{1,0:T(8,128)(2,1)} collective-permute-done((bf16[128,3072]{1,0:T(8,128)(2,1)S(1)}, bf16[128,3072]{1,0:T(8,128)(2,1)}, u32[]{:S(2)}, u32[]{:S(2)}) %collective-permute-start.3) | collective-permute-done | bytes 786464 | tf_op jit(solution)/shard_map/ppermute | solution.py:118
  46.4 2.6 collective-permute-start.4
  48.9 3.5 %collective-permute-start = (s32[256]{0:T(256)}, s32[256]{0:T(256)S(1)}, u32[]{:S(2)}, u32[]{:S(2)}) collective-permute-start(s32[256]{0:T(256)} %param.21), channel_id=1, source_target_pairs={{0,8},{8,16},{16,24},{24,32},{32,40},{40,48},{48,56},{56,64},{64,7... | collective-permute-start | bytes 3080 | tf_op jit(solution)/shard_map/ppermute | solution.py:15
  52.5 3.6 %collective-permute-start.9 = (bf16[2,256,128]{2,1,0:T(8,128)(2,1)}, bf16[2,256,128]{2,1,0:T(8,128)(2,1)S(1)}, u32[]{:S(2)}, u32[]{:S(2)}) collective-permute-start(bf16[2,256,128]{2,1,0:T(8,128)(2,1)} %param.20), channel_id=1, source_target_pairs={{0,8},{8,16},{16,24},{24,32},{32,40},{40,48},{48,56},{56,64},{64,7... | collective-permute-start | bytes 393224 | tf_op jit(solution)/shard_map/ppermute | solution.py:15
  58.2 2.5 collective-permute-start.5
  61.6 8.4 %collective-permute-done.5 = bf16[128,3072]{1,0:T(8,128)(2,1)} collective-permute-done((bf16[128,3072]{1,0:T(8,128)(2,1)}, bf16[128,3072]{1,0:T(8,128)(2,1)}, u32[]{:S(2)}, u32[]{:S(2)}) %collective-permute-start.5) | collective-permute-done | bytes 786464 | tf_op jit(solution)/shard_map/ppermute | solution.py:118
  69.9 2.5 collective-permute-start.6
  72.4 3.1 multiply_cosine_fusion
  75.5 6.1 %collective-permute-done.6 = bf16[128,3072]{1,0:T(8,128)(2,1)} collective-permute-done((bf16[128,3072]{1,0:T(8,128)(2,1)}, bf16[128,3072]{1,0:T(8,128)(2,1)}, u32[]{:S(2)}, u32[]{:S(2)}) %collective-permute-start.6) | collective-permute-done | bytes 786464 | tf_op jit(solution)/shard_map/ppermute | solution.py:118
  81.7 2.5 collective-permute-start.7
  86.6 7.5 %collective-permute-done.7 = bf16[128,3072]{1,0:T(8,128)(2,1)} collective-permute-done((bf16[128,3072]{1,0:T(8,128)(2,1)}, bf16[128,3072]{1,0:T(8,128)(2,1)}, u32[]{:S(2)}, u32[]{:S(2)}) %collective-permute-start.7) | collective-permute-done | bytes 786464 | tf_op jit(solution)/shard_map/ppermute | solution.py:118
  109.4 2.2 fusion.39
  112.8 2.2 fusion.45
  115.9 3.7 %collective-permute-start.8 = (bf16[2,1024,128]{1,2,0:T(8,128)(2,1)}, bf16[2,1024,128]{1,2,0:T(8,128)(2,1)}, u32[]{:S(2)}, u32[]{:S(2)}) collective-permute-start(bf16[2,1024,128]{1,2,0:T(8,128)(2,1)} %pad_maximum_fusion.1), channel_id=1, source_target_pairs={{0,8},{8,16},{16,24},{24,32},{32,40},{40,48},{48,56},{56,64},{64,7... | collective-permute-start | bytes 1572872 | tf_op jit(solution)/shard_map/ppermute | solution.py:15
  119.5 2.7 fusion.29
  123.3 2.8 copy.74
  126.0 1.6 copy.73
  127.7 2.6 subtract_convert_fusion
  132.4 6.1 %collective-permute-done.8 = bf16[2,1024,128]{1,2,0:T(8,128)(2,1)} collective-permute-done((bf16[2,1024,128]{1,2,0:T(8,128)(2,1)}, bf16[2,1024,128]{1,2,0:T(8,128)(2,1)}, u32[]{:S(2)}, u32[]{:S(2)}) %collective-permute-start.8) | collective-permute-done | bytes 524320 | tf_op jit(solution)/shard_map/ppermute | solution.py:15
  140.9 68.4 %while.14 = (s32[]{:T(128)}, f32[2,512,1,3]{1,0,3,2:T(2,128)S(1)}, f32[2,512,1,3]{1,0,2,3:T(2,128)S(1)}, f32[2,512,1,3,128]{4,1,0,3,2:T(8,128)}, s32[2]{0:T(128)...) while((s32[]{:T(128)}, f32[2,512,1,3]{1,0,3,2:T(2,128)S(1)}, ...), condition=%wide.region_9.10_spmd, body=%wide.region_6.9_spmd.sunk | while | flops 1650459648 | bytes 49834276 | solution.py:184
  142.3 1.6 compare_and_fusion.2
  143.9 2.1 constant_dynamic-slice_fusion.7
  146.0 1.9 copy.86
  147.9 8.1 %fusion.103 = (f32[512,3]{0,1:T(4,128)S(1)}, f32[2048,512,3]{1,0,2:T(8,128)}) fusion(pred[512,2048]{0,1:T(8,128)(4,1)S(1)} %compare_and_fusion.2, bf16[2,512,1,3,128]{4,1,0,3,2:T(8,128)(2,1)} %get-tuple-element.368, s32[]{:T(128)S(6)} %copy.112, bf16[512,1,128]{2,0,1:T(8,128)(2,1)} %get-tuple-element.367, bf16[1536,1,128]{2,0,1:T(8,128)(2,1)} %copy.86), kind=kOutput, calls=%fused_computation.4.clone.1 | convolution fusion | flops 815790592 | bytes 14555140 | tf_op jit(solution)/shard_map/while/body/eval_jaxpr/bgph,ngh->bgpn/dot_general | solution.py:60
  156.1 7.3 %fusion.104 = f32[512,3]{0,1:T(4,128)S(1)} fusion(f32[2048,512,3]{1,0,2:T(8,128)} %get-tuple-element.311, f32[512,3]{0,1:T(4,128)S(1)} %get-tuple-element.310, pred[512,2048]{0,1:T(8,128)(4,1)S(1)} %compare_and_fusion.2), kind=kLoop, calls=%fused_computation.3.clone.1 | loop fusion | flops 12581376 | bytes 13643776 | tf_op jit(solution)/shard_map/while/body/eval_jaxpr/reduce_sum | solution.py:68
  163.4 9.3 %fusion.105 = f32[1,512,1,3,128]{1,4,3,2,0:T(8,128)} fusion(f32[2048,512,3]{1,0,2:T(8,128)} %get-tuple-element.311, f32[512,3]{0,1:T(4,128)S(1)} %get-tuple-element.310, pred[512,2048]{0,1:T(8,128)(4,1)S(1)} %compare_and_fusion.2, bf16[512,1,128]{0,2,1:T(8,128)(2,1)} %get-tuple-element.370, bf16[1536,1,128]{0,2,1:T(8,128)(2,1)} %get-tuple-element.312), kind=kOutput, calls=%fused_computation.9.clone.1 | convolution fusion | flops 818937856 | bytes 14948352 | tf_op jit(solution)/shard_map/while/body/eval_jaxpr/bgpn,ngh->bgph/dot_general | solution.py:69
  172.7 1.4 copy.88
  176.5 1.6 compare_and_fusion.2
  178.1 2.1 constant_dynamic-slice_fusion.7
  180.2 1.9 copy.86
  182.1 8.1 %fusion.103 = (f32[512,3]{0,1:T(4,128)S(1)}, f32[2048,512,3]{1,0,2:T(8,128)}) fusion(pred[512,2048]{0,1:T(8,128)(4,1)S(1)} %compare_and_fusion.2, bf16[2,512,1,3,128]{4,1,0,3,2:T(8,128)(2,1)} %get-tuple-element.368, s32[]{:T(128)S(6)} %copy.112, bf16[512,1,128]{2,0,1:T(8,128)(2,1)} %get-tuple-element.367, bf16[1536,1,128]{2,0,1:T(8,128)(2,1)} %copy.86), kind=kOutput, calls=%fused_computation.4.clone.1 | convolution fusion | flops 815790592 | bytes 14555140 | tf_op jit(solution)/shard_map/while/body/eval_jaxpr/bgph,ngh->bgpn/dot_general | solution.py:60
  190.3 7.3 %fusion.104 = f32[512,3]{0,1:T(4,128)S(1)} fusion(f32[2048,512,3]{1,0,2:T(8,128)} %get-tuple-element.311, f32[512,3]{0,1:T(4,128)S(1)} %get-tuple-element.310, pred[512,2048]{0,1:T(8,128)(4,1)S(1)} %compare_and_fusion.2), kind=kLoop, calls=%fused_computation.3.clone.1 | loop fusion | flops 12581376 | bytes 13643776 | tf_op jit(solution)/shard_map/while/body/eval_jaxpr/reduce_sum | solution.py:68
  197.6 9.3 %fusion.105 = f32[1,512,1,3,128]{1,4,3,2,0:T(8,128)} fusion(f32[2048,512,3]{1,0,2:T(8,128)} %get-tuple-element.311, f32[512,3]{0,1:T(4,128)S(1)} %get-tuple-element.310, pred[512,2048]{0,1:T(8,128)(4,1)S(1)} %compare_and_fusion.2, bf16[512,1,128]{0,2,1:T(8,128)(2,1)} %get-tuple-element.370, bf16[1536,1,128]{0,2,1:T(8,128)(2,1)} %get-tuple-element.312), kind=kOutput, calls=%fused_computation.9.clone.1 | convolution fusion | flops 818937856 | bytes 14948352 | tf_op jit(solution)/shard_map/while/body/eval_jaxpr/bgpn,ngh->bgph/dot_general | solution.py:69
  209.3 2.6 slice.77
  211.9 3.0 copy.54
  215.1 12.5 %fusion.92 = (f32[64,3]{0,1:T(4,128)S(1)}, f32[64,1,3,32768]{3,0,2,1:T(8,128)}) fusion(bf16[2,32768,128]{2,1,0:T(8,128)(2,1)} %all-gather.2.cloned.1.call-done, bf16[1024,3,64]{2,0,1:T(8,128)(2,1)} %copy-done.3, bf16[1024,3,64]{2,0,1:T(8,128)(2,1)} %copy-done.2), kind=kOutput, calls=%fused_computation.149 | convolution fusion | flops 1623293696 | bytes 35128064 | tf_op jit(solution)/shard_map/bgph,ngh->bgpn/dot_general | solution.py:60
  227.6 10.6 %fusion.23 = f32[64,3]{0,1:T(4,128)S(1)} fusion(f32[64,1,3,32768]{3,0,2,1:T(8,128)} %get-tuple-element.201, f32[64,3]{0,1:T(4,128)S(1)} %get-tuple-element.200), kind=kLoop, calls=%fused_computation.34 | loop fusion | flops 12582720 | bytes 25167360 | tf_op jit(solution)/shard_map/reduce_sum | solution.py:68
  238.2 14.4 %fusion.63 = f32[64,1,3,128]{3,0,2,1:T(8,128)S(1)} fusion(bf16[2,32768,128]{2,1,0:T(8,128)(2,1)} %all-gather.2.cloned.1.call-done, f32[64,1,3,32768]{3,0,2,1:T(8,128)} %get-tuple-element.201, f32[64,3]{0,1:T(4,128)S(1)} %get-tuple-element.200, f32[1024,1,3,128]{3,0,2,1:T(8,128)} %bitcast.186, f32[64,3]{0,1:T(4,128)S(1)} %bitcast.193, ...), kind=kOutput, calls=%fused_computation.65 | convolution fusion | flops 1623318528 | bytes 33754880 | tf_op jit(solution)/shard_map/bgpn,ngh->bgph/dot_general | solution.py:69
  252.9 1.9 fusion.38
  254.8 5.5 %convolution_convert_fusion = bf16[1024,3072]{1,0:T(8,128)(2,1)} fusion(bf16[1024,384]{0,1:T(8,128)(2,1)S(1)} %fusion.38, bf16[384,3072]{1,0:T(8,128)(2,1)S(1)} %copy-done), kind=kOutput, calls=%fused_computation.41 | convolution fusion | flops 2419064832 | bytes 9437184 | tf_op jit(solution)/shard_map/dot_general | solution.py:218
  260.3 56.6 %reduce-scatter.2.cloned.1.call-done = bf16[128,3072]{1,0:T(8,128)(2,1)} async-done(((bf16[1024,3072]{1,0:T(8,128)(2,1)}), bf16[128,3072]{1,0:T(8,128)(2,1)}) %reduce-scatter.2.cloned.1.call-update) | async-done | bytes 786448 | tf_op jit(solution)/shard_map/reduce_scatter | solution.py:217
  (117 shorter events, 36.2 us)
Async XLA Ops:
  6.5 248.3 %copy-start = (bf16[384,3072]{1,0:T(8,128)(2,1)S(1)}, bf16[384,3072]{1,0:T(8,128)(2,1)}, u32[]{:S(2)}) copy-start(bf16[384,3072]{1,0:T(8,128)(2,1)} %param.18) | copy-start | bytes 7077892
  6.5 96.1 %copy-start.1 = (bf16[128,3072]{1,0:T(8,128)(2,1)S(1)}, bf16[128,3072]{1,0:T(8,128)(2,1)}, u32[]{:S(2)}) copy-start(bf16[128,3072]{1,0:T(8,128)(2,1)} %param.13) | copy-start | bytes 2359300
  6.5 96.1 %copy-start.9 = (f32[3072]{0:T(1024)S(1)}, f32[3072]{0:T(1024)}, u32[]{:S(2)}) copy-start(f32[3072]{0:T(1024)} %param.14) | copy-start | bytes 36868
  6.5 208.5 %all-gather.2.cloned.1.call-start = ((), (), s32[]{:S(2)}) async-start(), calls=%async_computation.1 | async-start | bytes 17301504 | tf_op jit(solution)/shard_map/all_gather | solution.py:202
  7.3 309.7 %reduce-scatter.2.cloned.1.call-start = ((), (), s32[]{:S(2)}) async-start(), calls=%async_computation.2 | async-start | bytes 7077888 | tf_op jit(solution)/shard_map/reduce_scatter | solution.py:217
  10.1 11.6 %collective-permute-start.1 = (bf16[128,3072]{1,0:T(8,128)(2,1)S(1)}, bf16[128,3072]{1,0:T(8,128)(2,1)S(1)}, u32[]{:S(2)}, u32[]{:S(2)}) collective-permute-start(bf16[128,3072]{1,0:T(8,128)(2,1)S(1)} %fusion.37), channel_id=1, source_target_pairs={{0,1},{1,2},{2,3},{3,4},{4,5},{5,6},{6,7},{7,0},{8,9},{9,10},{10,1... | collective-permute-start | bytes 2359304 | tf_op jit(solution)/shard_map/ppermute | solution.py:118
  21.8 0.9 copy-start.4
  22.6 11.4 %collective-permute-start.2 = (bf16[128,3072]{1,0:T(8,128)(2,1)S(1)}, bf16[128,3072]{1,0:T(8,128)(2,1)S(1)}, u32[]{:S(2)}, u32[]{:S(2)}) collective-permute-start(bf16[128,3072]{1,0:T(8,128)(2,1)S(1)} %collective-permute-done.1), channel_id=1, source_target_pairs={{0,1},{1,2},{2,3},{3,4},{4,5},{5,6},{6,7},{7,0},{8,9},{9,10},{10,1... | collective-permute-start | bytes 2359304 | tf_op jit(solution)/shard_map/ppermute | solution.py:118
  34.1 0.9 copy-start.6
  34.9 11.4 %collective-permute-start.3 = (bf16[128,3072]{1,0:T(8,128)(2,1)S(1)}, bf16[128,3072]{1,0:T(8,128)(2,1)}, u32[]{:S(2)}, u32[]{:S(2)}) collective-permute-start(bf16[128,3072]{1,0:T(8,128)(2,1)S(1)} %collective-permute-done.2), channel_id=1, source_target_pairs={{0,1},{1,2},{2,3},{3,4},{4,5},{5,6},{6,7},{7,0},{8,9},{9,10},{10,1... | collective-permute-start | bytes 2359304 | tf_op jit(solution)/shard_map/ppermute | solution.py:118
  46.4 11.8 %collective-permute-start.4 = (bf16[128,3072]{1,0:T(8,128)(2,1)}, bf16[128,3072]{1,0:T(8,128)(2,1)}, u32[]{:S(2)}, u32[]{:S(2)}) collective-permute-start(bf16[128,3072]{1,0:T(8,128)(2,1)} %collective-permute-done.3), channel_id=1, source_target_pairs={{0,1},{1,2},{2,3},{3,4},{4,5},{5,6},{6,7},{7,0},{8,9},{9,10},{10,1... | collective-permute-start | bytes 2359304 | tf_op jit(solution)/shard_map/ppermute | solution.py:118
  48.9 35.2 %collective-permute-start = (s32[256]{0:T(256)}, s32[256]{0:T(256)S(1)}, u32[]{:S(2)}, u32[]{:S(2)}) collective-permute-start(s32[256]{0:T(256)} %param.21), channel_id=1, source_target_pairs={{0,8},{8,16},{16,24},{24,32},{32,40},{40,48},{48,56},{56,64},{64,7... | collective-permute-start | bytes 3080 | tf_op jit(solution)/shard_map/ppermute | solution.py:15
  52.5 31.7 %collective-permute-start.9 = (bf16[2,256,128]{2,1,0:T(8,128)(2,1)}, bf16[2,256,128]{2,1,0:T(8,128)(2,1)S(1)}, u32[]{:S(2)}, u32[]{:S(2)}) collective-permute-start(bf16[2,256,128]{2,1,0:T(8,128)(2,1)} %param.20), channel_id=1, source_target_pairs={{0,8},{8,16},{16,24},{24,32},{32,40},{40,48},{48,56},{56,64},{64,7... | collective-permute-start | bytes 393224 | tf_op jit(solution)/shard_map/ppermute | solution.py:15
  58.2 11.7 %collective-permute-start.5 = (bf16[128,3072]{1,0:T(8,128)(2,1)}, bf16[128,3072]{1,0:T(8,128)(2,1)}, u32[]{:S(2)}, u32[]{:S(2)}) collective-permute-start(bf16[128,3072]{1,0:T(8,128)(2,1)} %collective-permute-done.4), channel_id=1, source_target_pairs={{0,1},{1,2},{2,3},{3,4},{4,5},{5,6},{6,7},{7,0},{8,9},{9,10},{10,1... | collective-permute-start | bytes 2359304 | tf_op jit(solution)/shard_map/ppermute | solution.py:118
  69.9 11.7 %collective-permute-start.6 = (bf16[128,3072]{1,0:T(8,128)(2,1)}, bf16[128,3072]{1,0:T(8,128)(2,1)}, u32[]{:S(2)}, u32[]{:S(2)}) collective-permute-start(bf16[128,3072]{1,0:T(8,128)(2,1)} %collective-permute-done.5), channel_id=1, source_target_pairs={{0,1},{1,2},{2,3},{3,4},{4,5},{5,6},{6,7},{7,0},{8,9},{9,10},{10,1... | collective-permute-start | bytes 2359304 | tf_op jit(solution)/shard_map/ppermute | solution.py:118
  81.7 12.4 %collective-permute-start.7 = (bf16[128,3072]{1,0:T(8,128)(2,1)}, bf16[128,3072]{1,0:T(8,128)(2,1)}, u32[]{:S(2)}, u32[]{:S(2)}) collective-permute-start(bf16[128,3072]{1,0:T(8,128)(2,1)} %collective-permute-done.6), channel_id=1, source_target_pairs={{0,1},{1,2},{2,3},{3,4},{4,5},{5,6},{6,7},{7,0},{8,9},{9,10},{10,1... | collective-permute-start | bytes 2359304 | tf_op jit(solution)/shard_map/ppermute | solution.py:118
  86.6 22.4 %copy-start.7 = (bf16[128,3072]{1,0:T(8,128)(2,1)S(1)}, bf16[128,3072]{1,0:T(8,128)(2,1)}, u32[]{:S(2)}) copy-start(bf16[128,3072]{1,0:T(8,128)(2,1)} %copy-done.6) | copy-start | bytes 2359300
  86.6 22.5 %copy-start.5 = (bf16[128,3072]{1,0:T(8,128)(2,1)S(1)}, bf16[128,3072]{1,0:T(8,128)(2,1)}, u32[]{:S(2)}) copy-start(bf16[128,3072]{1,0:T(8,128)(2,1)} %copy-done.4) | copy-start | bytes 2359300
  86.6 22.8 %copy-start.12 = (bf16[3072,128]{1,0:T(8,128)(2,1)S(1)}, bf16[3072,128]{1,0:T(8,128)(2,1)}, u32[]{:S(2)}) copy-start(bf16[3072,128]{1,0:T(8,128)(2,1)} %param.16) | copy-start | bytes 2359300
  101.4 11.4 %copy-start.13 = (bf16[3072,128]{1,0:T(8,128)(2,1)S(1)}, bf16[3072,128]{1,0:T(8,128)(2,1)}, u32[]{:S(2)}) copy-start(bf16[3072,128]{1,0:T(8,128)(2,1)} %param.17) | copy-start | bytes 2359300
  109.0 10.6 %copy-start.11 = (bf16[3072,384]{1,0:T(8,128)(2,1)S(1)}, bf16[3072,384]{1,0:T(8,128)(2,1)}, u32[]{:S(2)}) copy-start(bf16[3072,384]{1,0:T(8,128)(2,1)} %param.15) | copy-start | bytes 7077892
  115.0 0.9 copy-start.8
  115.9 22.7 %collective-permute-start.8 = (bf16[2,1024,128]{1,2,0:T(8,128)(2,1)}, bf16[2,1024,128]{1,2,0:T(8,128)(2,1)}, u32[]{:S(2)}, u32[]{:S(2)}) collective-permute-start(bf16[2,1024,128]{1,2,0:T(8,128)(2,1)} %pad_maximum_fusion.1), channel_id=1, source_target_pairs={{0,8},{8,16},{16,24},{24,32},{32,40},{40,48},{48,56},{56,64},{64,7... | collective-permute-start | bytes 1572872 | tf_op jit(solution)/shard_map/ppermute | solution.py:15
  122.2 18.7 %copy-start.10 = (s32[256]{0:T(256)S(1)}, s32[256]{0:T(256)}, u32[]{:S(2)}) copy-start(s32[256]{0:T(256)} %param.21) | copy-start | bytes 3076
  130.2 0.9 copy-start.2
  130.2 2.2 copy-start.3
Sparse Core Ops, SparseCore 0:
  10.0 154.8 all-gather.1
  260.4 56.4 reduce-scatter.1
